TPU v7x, 32 devices: a whole 2x2x4 slice. The times are simulated.
32 devices in a mesh: gx: 8 (over y, x, core), gy: 4 (over z).
Axes of the slice: x: 2, y: 2, z: 4, core: 2. Of those that a mesh axis runs over, the one named last changes fastest.
Arguments:
- west_in: float32 [2, 32, 256, 128], P(None, 'gx', 'gy'), may hold values from -6 to 6
- south_in: float32 [2, 256, 16, 128], P(None, 'gx', 'gy'), may hold values from -6 to 6
- region: int32 [256, 256], P('gx', 'gy'), may hold values from 0 to 7
- pml_layers: int32 [4, 8, 4], P(None, 'gx', 'gy'), may hold values from 0 to 8
- vel_table: float32 [8, 128], replicated, may hold values from 0.3 to 3
- src_slot: int32 [8, 4], P('gx', 'gy'), may hold values from 0 to 12
- src_cell: int32 [8, 4], P('gx', 'gy'), may hold values from 0 to 262143
- src_amp: float32 [2, 13], replicated, may hold values from -16 to 16
- wave_sq: float32 [], replicated, may hold values from 0.5 to 2
Outputs:
- fields: bfloat16 [3, 2, 256, 256, 128], P(None, None, 'gx', 'gy')
All inputs are finite; a program needn't handle non-finite values.
Results may differ from a plain program's by a relative error of at most 0.001.
Values sent between devices are 32-bit elements; how exact they have to be, the bound alone decides.
A program may use at most 64 MiB of HBM per device.

v0:
```python
import functools

import jax
import jax.numpy as jnp
import numpy as np
from jax import lax
from jax.experimental import pallas as pl
from jax.experimental.pallas import tpu as pltpu
from jax.sharding import PartitionSpec as P

DEPTH = 4
TICKS = 3
PIECES = 4
INNER_PIECES = 3
SUB = 8
damping_ratio = 0.25
absorb_peak = 4.0
diagonal_base = 6.0
F32 = jnp.float32
BF16 = jnp.bfloat16
MESH = pl.DeviceIdType.MESH


def basis(count):
    k = np.arange(count, dtype=np.float64) + 1.0
    table = np.sqrt(2.0 / (count + 1.0)) * np.sin(np.pi * k[:, None] * k[None, :] / (count + 1.0))
    eigen = 2.0 - 2.0 * np.cos(np.pi * k / (count + 1.0))
    return table, eigen


def np_split(table):
    full = np.asarray(table, np.float32)
    high = full.astype(BF16)
    low = (full - high.astype(np.float32)).astype(BF16)
    return high, low


def left3(table):
    high, low = np_split(table)
    return np.concatenate([high, high, low], axis=1)


def fold(table):
    high, low = np_split(table)
    return np.concatenate([np.concatenate([high, high], 1), np.concatenate([low, np.zeros_like(low)], 1)], 0)


def edges_first(table, depth):
    rows = table.shape[0] // 2
    cut = depth * SUB
    return np.concatenate([table[:cut], table[rows:rows + cut], table[cut:rows], table[rows + cut:]], axis=0)


def segments(sx):
    inner = (sx - 2 * DEPTH) // INNER_PIECES
    bounds = [(0, DEPTH), (sx - DEPTH, sx)]
    return bounds + [(DEPTH + k * inner, DEPTH + (k + 1) * inner) for k in range(INNER_PIECES)]


def split(values):
    high = values.astype(BF16).astype(F32)
    return high, values - high


def right3(values):
    high, low = split(values)
    high = high.astype(BF16)
    return jnp.concatenate([high, low.astype(BF16), high], axis=0)


def right2(values):
    high, low = split(values)
    return jnp.concatenate([high.astype(BF16), low.astype(BF16)], axis=0)


def mm(a, b):
    return jnp.dot(a, b, preferred_element_type=F32)


def halves(both):
    size = both.shape[0] // 2
    return both[:size] + both[size:]


def along_z(values, zz):
    high, low = split(values)
    both = jnp.concatenate([high.astype(BF16), low.astype(BF16)], axis=1)
    out = mm(both, zz)
    half = out.shape[1] // 2
    return out[:, :half] + out[:, half:]


def make_tables(sx, sy, sz):
    bx, ex = basis(sx)
    by, ey = basis(sy)
    bz, ez = basis(sz)
    eye = np.eye(SUB)
    groups = sy // SUB
    ls = [np_split(np.kron(np.eye(sx), by[g * SUB:(g + 1) * SUB, :DEPTH])) for g in range(groups)]
    lsh = np.stack([np.concatenate([h, h], axis=1) for h, _ in ls])
    lsl = np.stack([low for _, low in ls])
    half = sx // 2
    order = np.concatenate([np.arange(0, sx, 2), np.arange(1, sx, 2)])
    bxo, exo = bx[order], ex[order]
    lw = left3(np.kron(bxo[:, :DEPTH], eye))
    lw = np.concatenate([lw, np.zeros((lw.shape[0], 4 * SUB), lw.dtype)], axis=1)
    zh, zl = np_split(bz)
    zz = np.concatenate([np.concatenate([zh, zl], 1)] * 2, 0)
    return dict(
        lsh=lsh.reshape(groups // 2, -1, lsh.shape[2]),
        lsl=lsl,
        lw=lw,
        te=edges_first(fold(np.kron(bx[:half, order[:half]], eye)), DEPTH),
        to=edges_first(fold(np.kron(bx[:half, order[half:]], eye)), DEPTH),
        ts=left3(np.kron(bxo, np.eye(DEPTH))),
        ty=fold(by),
        zz=zz,
        bxr=np.repeat(bxo, SUB, axis=0).astype(np.float32),
        byf=by.astype(np.float32),
        bzf=bz.astype(np.float32),
        exr=np.repeat(exo, SUB)[:, None].astype(np.float32) * np.ones((1, sz), np.float32),
        eyr=ey[:, None].astype(np.float32) * np.ones((1, sz), np.float32),
        ezr=ez[None, :].astype(np.float32),
    )


SCALARS = ("pml", "amp", "wave")
INVERSE_UNROLL = 2
NAMES = ("lsh", "lsl", "lw", "te", "to", "ts", "ty", "zz", "bxr", "byf", "bzf", "exr", "eyr", "ezr")


INPUTS = SCALARS + ("west_in", "south_in", "region", "vel") + NAMES
FIRST = ("wave", "ezr", "eyr", "exr", "bxr", "byf", "bzf", "lw", "pml", "region", "vel")
ORDER = FIRST + tuple(name for name in INPUTS if name not in FIRST)


def finish_plane(x, mid, mult, ty):
    sz = mid.shape[3]
    plane = jnp.concatenate([mid[0, x], mid[1, x]], axis=1)
    raw = halves(mm(ty[...], right2(plane)))
    re, im = raw[:, :sz], raw[:, sz:]
    mr, mi = mult[0, x], mult[1, x]
    fr = re + mr * re - mi * im
    fi = im + mr * im + mi * re
    return fr, fi


def finish(early, mid, mult, ty, out, last, sems):
    sx = mid.shape[1]
    count = early.shape[0]
    copies = [pltpu.make_async_copy(early.at[t], out.at[t], sems.at[t]) for t in range(count)]
    for copy in copies:
        copy.start()
    size = sx // PIECES
    for k in range(PIECES):
        for x in range(k * size, (k + 1) * size):
            fr, fi = finish_plane(x, mid, mult, ty)
            last[0, x] = fr.astype(BF16)
            last[1, x] = fi.astype(BF16)
        part = pl.ds(k * size, size)
        copy = pltpu.make_async_copy(last.at[:, part], out.at[count, :, part], sems.at[count + k])
        copy.start()
        copies.append(copy)
    for copy in copies:
        copy.wait()


def kernel(n_gx, n_gy, *refs):
    slot, cell = refs[:2]
    outside, (obuf, mid, mult), refs = refs[2:23], refs[23:26], refs[26:]
    inside, refs = refs[:21], refs[21:]
    pml, amp, wave = inside[:3]
    (west_in, south_in, region, vel,
     lsh, lsl, lw0, te, to, ts, ty, zz, bxr, byf, bzf, exr, eyr, ezr) = inside[3:]
    (
     west_buf, south_buf, east_buf, north_buf,
     lw, point, pq, reg2, ab, rs, wf, sp,
     send_e, recv_w, send_n, recv_s, load_sem) = refs
    sx, sy = region.shape
    sz = vel.shape[1]
    labels = vel.shape[0]
    groups = sy // SUB
    span = sx * SUB
    a = lax.axis_index("gx")
    b = lax.axis_index("gy")
    has_w, has_e = a > 0, a + 1 < n_gx
    has_s, has_n = b > 0, b + 1 < n_gy

    loads = {name: pltpu.make_async_copy(src, dst, load_sem.at[i])
             for i, (name, (src, dst)) in enumerate(zip(INPUTS, zip(outside, inside)))}
    for name in ORDER:
        loads[name].start()

    def need(*names):
        for name in names:
            loads[name].wait()

    barrier = pltpu.get_barrier_semaphore()

    @pl.when(has_w)
    def _():
        pl.semaphore_signal(barrier, inc=1, device_id=(a - 1, b), device_id_type=MESH)

    @pl.when(has_s)
    def _():
        pl.semaphore_signal(barrier, inc=1, device_id=(a, b - 1), device_id_type=MESH)


    @pl.when(jnp.logical_not(has_w))
    def _():
        west_buf[...] = jnp.zeros_like(west_buf)

    @pl.when(jnp.logical_not(has_s))
    def _():
        south_buf[...] = jnp.zeros_like(south_buf)

    need("wave", "exr", "eyr", "ezr")
    w = wave[0, 0]
    damp = -damping_ratio * w

    def inverse_group(g, carry):
        y_part = eyr[pl.ds(pl.multiple_of(g * SUB, SUB), SUB), :]
        lam = exr[...].reshape(sx, SUB, sz) + y_part[None] + ezr[...][None] - w
        lam = lam.reshape(sx * SUB, sz)
        inv = 1.0 / (lam * lam + damp * damp)
        pq[0, g] = lam * inv
        pq[1, g] = damp * inv
        return carry

    lax.fori_loop(0, groups, inverse_group, 0, unroll=INVERSE_UNROLL)
    need("bxr", "byf", "bzf", "lw")

    position = cell[0, 0]
    px = position // (sy * sz)
    py = (position // sz) % sy
    pz = position % sz
    x_lane = lax.broadcasted_iota(jnp.int32, (sx * SUB, sx), 1)
    bxp = jnp.sum(jnp.where(x_lane == px, bxr[...], 0.0), axis=1, keepdims=True)
    y_lane = lax.broadcasted_iota(jnp.int32, (sy, sy), 1)
    byp = jnp.sum(jnp.where(y_lane == py, byf[...], 0.0), axis=1, keepdims=True)
    z_row = lax.broadcasted_iota(jnp.int32, (sz, sz), 0)
    bzp = jnp.sum(jnp.where(z_row == pz, bzf[...], 0.0), axis=0, keepdims=True)
    point[...] = byp * bzp
    width = lw0.shape[1]
    first = 3 * DEPTH * SUB
    lane = lax.broadcasted_iota(jnp.int32, (sx * SUB, width), 1)
    row = lax.broadcasted_iota(jnp.int32, (sx * SUB, width), 0)
    xh, xl = split(bxp)
    dyn = jnp.where(lane < first + 2 * SUB, xh, xl)
    dyn = jnp.where((lane % SUB) == (row % SUB), dyn, 0.0)
    lw[...] = jnp.where(lane < first, lw0[...].astype(F32), dyn).astype(BF16)

    xi = lax.broadcasted_iota(jnp.int32, (sx, 2 * sy), 0).astype(F32)
    lane2 = lax.broadcasted_iota(jnp.int32, (sx, 2 * sy), 1)
    yi = (lane2 % sy).astype(F32)

    need("pml", "region", "vel")

    def ramp(i, distance):
        thick = pml[0, i].astype(F32)
        portion = jnp.maximum(thick - distance, 0.0) / jnp.maximum(jnp.full_like(distance, thick), 1.0)
        return portion * portion

    sigma = ramp(0, xi) + ramp(1, sx - 1.0 - xi) + ramp(2, yi) + ramp(3, sy - 1.0 - yi)
    sigma = absorb_peak * sigma
    den = diagonal_base * diagonal_base + sigma * sigma
    ab[...] = jnp.where(lane2 < sy, diagonal_base, -sigma) / den
    reg2[...] = jnp.concatenate([region[...], region[...]], axis=1)
    ch, cl = split(vel[...] - w)
    contrast = jnp.concatenate([ch, ch, cl, cl], axis=0).astype(BF16)
    label = lax.broadcasted_iota(jnp.int32, (labels, 2 * sy), 0)

    def mult_plane(x, carry):
        own = jnp.where(reg2[pl.ds(x, 1), :] == label, ab[pl.ds(x, 1), :], 0.0)
        oh, ol = split(own)
        lhs = jnp.concatenate([oh, ol, oh, ol], axis=0).astype(BF16)
        res = lax.dot_general(lhs, contrast, (((0,), (0,)), ((), ())), preferred_element_type=F32)
        mult[0, x] = res[:sy]
        mult[1, x] = res[sy:]
        return carry

    lax.fori_loop(0, sx, mult_plane, 0, unroll=8)

    @pl.when(jnp.logical_and(has_e, has_n))
    def _():
        pl.semaphore_wait(barrier, 2)

    @pl.when(jnp.logical_xor(has_e, has_n))
    def _():
        pl.semaphore_wait(barrier, 1)

    def east_copy(t, p):
        return pltpu.make_async_remote_copy(
            src_ref=east_buf.at[t, :, pl.ds(2 * p, 2)], dst_ref=west_buf.at[t, :, pl.ds(2 * p, 2)],
            send_sem=send_e.at[t, p], recv_sem=recv_w.at[t, p],
            device_id=(a + 1, b), device_id_type=MESH)

    spans = segments(sx)

    def north_copy(t, k):
        rows = pl.ds(spans[k][0] * DEPTH, (spans[k][1] - spans[k][0]) * DEPTH)
        return pltpu.make_async_remote_copy(
            src_ref=north_buf.at[t, :, rows, :], dst_ref=south_buf.at[t, :, rows, :],
            send_sem=send_n.at[t, k], recv_sem=recv_s.at[t, k],
            device_id=(a, b + 1), device_id_type=MESH)

    def spread(q, even_in, odd_in, low, high):
        whole = low == 0 and high == sx // 2

        def planes(table, values):
            if not whole:
                return halves(mm(table[2 * low * SUB:2 * high * SUB, :], values))
            out = mm(table[...], values)
            edge = 2 * DEPTH * SUB
            return jnp.concatenate([halves(out[:edge]), halves(out[edge:])], axis=0)

        even = planes(te, even_in)
        odd = planes(to, odd_in)
        res = jnp.concatenate([even + odd, even - odd], axis=0)
        size = res.shape[0]
        done = along_z(jnp.concatenate([res[:, n * sz:(n + 1) * sz] for n in range(4)], axis=0), zz[...])
        count = high - low
        for k in range(2):
            rows = pl.ds((2 * q + k) * SUB, SUB)
            for c in range(2):
                n = 2 * k + c
                block = done[n * size:(n + 1) * size].reshape(2 * count, SUB, sz)
                mid[c, low:high, rows, :] = block[:count]
                for i in range(count):
                    mid[c, sx - 1 - low - i, rows, :] = block[count + i]

    need("west_in", "south_in", "ty", "zz", "ts")
    zpad = jnp.zeros((SUB, sz), F32)
    row8 = lax.broadcasted_iota(jnp.int32, (SUB, sz), 0)

    for t in range(TICKS):
        west = west_in if t == 0 else west_buf.at[t - 1]
        south = south_in if t == 0 else south_buf.at[t - 1]
        def take_west(p):
            if t > 0:
                @pl.when(has_w)
                def _():
                    east_copy(t - 1, p).wait_recv()

            planes = []
            for j in range(2 * p, 2 * p + 2):
                plane = jnp.concatenate([west[0, j], west[1, j]], axis=1)
                planes.append(halves(mm(ty[...], right2(plane))))
            rows = [q[:, c * sz:(c + 1) * sz] for c in range(2) for q in planes]
            done = along_z(jnp.concatenate(rows, axis=0), zz[...])
            wf[:, 2 * p:2 * p + 2] = done.reshape(2, 2, sy, sz)

        def take_south(parts):
            if t > 0:
                @pl.when(has_s)
                def _():
                    for k in parts:
                        north_copy(t - 1, k).wait_recv()

            cuts = [slice(spans[k][0] * DEPTH, spans[k][1] * DEPTH) for k in parts]
            done = along_z(jnp.concatenate([south[c, rows, :] for c in range(2) for rows in cuts], axis=0), zz[...])
            size = done.shape[0] // 2
            both = jnp.concatenate([done[:size], done[size:]], axis=1)
            at = 0
            for k, rows in zip(parts, cuts):
                step = rows.stop - rows.start
                arrived[k] = both[at:at + step]
                at += step

        arrived = {}
        every = list(range(len(spans)))
        take_west(0)
        if t == 0:
            take_south(every)
            take_west(1)
        else:
            take_west(1)
            take_south(every[:2])
            for k in every[2:]:
                take_south([k])
        in_order = sorted(every, key=lambda k: spans[k][0])
        rs[...] = right2(mm(ts[...], right3(jnp.concatenate([arrived[k] for k in in_order], axis=0))))

        if t == 0:
            need("lsh", "lsl", "te", "to", "amp")

        source = t - a - b + (n_gx + n_gy - 2)
        live = jnp.where(slot[0, 0] == source, 1.0, 0.0).astype(F32)
        amps = (amp[0, source] * live, amp[1, source] * live)

        def spectrum(q):
            shared = mm(lsh[q], rs[...])
            specs = []
            for k in range(2):
                g = 2 * q + k
                rows = pl.ds(g * SUB, SUB)
                p = point[rows, :]
                parts = []
                for c in range(2):
                    wh, wl = split(wf[c, :, rows, :].reshape(DEPTH * SUB, sz))
                    ph, pw = split(p * amps[c])
                    parts.append(jnp.concatenate([wh, wl, wh, ph, pw, ph, zpad], axis=0).astype(BF16))
                rw = jnp.concatenate([rs[: sx * DEPTH, :], jnp.concatenate(parts, axis=1)], axis=0)
                lhs = jnp.concatenate([lsl[g], lw[...]], axis=1)
                coeffs = shared[k * span:(k + 1) * span] + mm(lhs, rw)
                c0, c1 = coeffs[:, :sz], coeffs[:, sz:]
                pr, qr = pq[0, g], pq[1, g]
                specs += [c0 * pr + c1 * qr, c1 * pr - c0 * qr]
            spec = jnp.concatenate(specs, axis=1)
            return right2(spec[: span // 2]), right2(spec[span // 2:])

        ahead = spectrum(0)
        for q in range(groups // 2):
            even_in, odd_in = ahead
            if q + 1 < groups // 2:
                ahead = spectrum(q + 1)
            if t + 1 == TICKS:
                spread(q, even_in, odd_in, 0, sx // 2)
            else:
                sp[2 * q] = even_in
                sp[2 * q + 1] = odd_in
                spread(q, even_in, odd_in, 0, DEPTH)

        if t + 1 == TICKS:
            break

        def one_plane(x):
            fr, fi = finish_plane(x, mid, mult, ty)
            obuf[t, 0, x] = fr.astype(BF16)
            obuf[t, 1, x] = fi.astype(BF16)
            return fr, fi

        def two_planes(i, east):
            first = one_plane(2 * i)
            second = one_plane(2 * i + 1)
            if t + 1 < TICKS:
                rows = pl.ds(pl.multiple_of(i * SUB, SUB), SUB)
                for c in range(2):
                    one = pltpu.roll(first[c][sy - SUB:], DEPTH, 0)
                    north_buf[t, c, rows, :] = jnp.where(row8 < DEPTH, one, second[c][sy - SUB:])
                    if east is not None:
                        east_buf[t, c, 2 * i - (sx - DEPTH)] = first[c]
                        east_buf[t, c, 2 * i + 1 - (sx - DEPTH)] = second[c]

        for i in range((sx - DEPTH) // 2, sx // 2):
            two_planes(i, True)

            @pl.when(has_e)
            def _():
                east_copy(t, i - (sx - DEPTH) // 2).start()

        for i in range(DEPTH // 2):
            two_planes(i, None)

        @pl.when(has_n)
        def _():
            north_copy(t, 0).start()
            north_copy(t, 1).start()

        for q in range(groups // 2):
            spread(q, sp[2 * q], sp[2 * q + 1], DEPTH, sx // 2)

        for k in range(2, len(spans)):
            for i in range(spans[k][0] // 2, spans[k][1] // 2):
                two_planes(i, None)

            @pl.when(has_n)
            def _():
                north_copy(t, k).start()

    for t in range(TICKS - 1):
        if t + 1 < TICKS:
            @pl.when(has_e)
            def _():
                for p in range(DEPTH // 2):
                    east_copy(t, p).wait_send()

            @pl.when(has_n)
            def _():
                for k in range(len(spans)):
                    north_copy(t, k).wait_send()


def solution(mesh):
    n_gx = mesh.shape["gx"]
    n_gy = mesh.shape["gy"]

    def local(west_in, south_in, region, pml_layers, vel_table, src_slot, src_cell, src_amp, wave_sq):
        sx, sy = region.shape
        sz = vel_table.shape[1]
        groups = sy // SUB
        consts = make_tables(sx, sy, sz)
        smem = pl.BlockSpec(memory_space=pltpu.SMEM)
        vmem = pl.BlockSpec(memory_space=pltpu.VMEM)
        hbm = pl.BlockSpec(memory_space=pl.ANY)
        dma = pltpu.SemaphoreType.DMA
        shape = (TICKS, 2, sx, sy, sz)
        inputs = [
            pml_layers.transpose(1, 2, 0).reshape(1, 4), src_amp, wave_sq.reshape(1, 1),
            west_in, south_in.reshape(2, sx * DEPTH, sz), region, vel_table,
            *[jnp.asarray(consts[name]) for name in NAMES],
        ]
        count = len(SCALARS)
        held = [pltpu.SMEM(v.shape, v.dtype) for v in inputs[:count]]
        held += [pltpu.VMEM(v.shape, v.dtype) for v in inputs[count:]]
        early, mid, mult = pl.pallas_call(
            functools.partial(kernel, n_gx, n_gy),
            out_shape=(
                pltpu.VMEM((TICKS - 1,) + shape[1:], BF16),
                pltpu.VMEM(shape[1:], F32),
                pltpu.VMEM(shape[1:], F32),
            ),
            in_specs=[smem] * 2 + [pl.BlockSpec(memory_space=pltpu.HBM)] * len(inputs),
            out_specs=(vmem,) * 3,
            scratch_shapes=held + [
                pltpu.VMEM((TICKS - 1, 2, DEPTH, sy, sz), F32),
                pltpu.VMEM((TICKS - 1, 2, sx * DEPTH, sz), F32),
                pltpu.VMEM((TICKS - 1, 2, DEPTH, sy, sz), F32),
                pltpu.VMEM((TICKS - 1, 2, sx * DEPTH, sz), F32),
                pltpu.VMEM(consts["lw"].shape, BF16),
                pltpu.VMEM((sy, sz), F32),
                pltpu.VMEM((2, groups, sx * SUB, sz), F32),
                pltpu.VMEM((sx, 2 * sy), jnp.int32),
                pltpu.VMEM((sx, 2 * sy), F32),
                pltpu.VMEM((2 * sx * DEPTH, 2 * sz), BF16),
                pltpu.VMEM((2, DEPTH, sy, sz), F32),
                pltpu.VMEM((groups, sx * SUB, 4 * sz), BF16),
                dma((TICKS - 1, DEPTH // 2)),
                dma((TICKS - 1, DEPTH // 2)),
                dma((TICKS - 1, INNER_PIECES + 2)),
                dma((TICKS - 1, INNER_PIECES + 2)),
                dma((len(inputs),)),
            ],
            compiler_params=pltpu.CompilerParams(
                collective_id=0, has_side_effects=True, vmem_limit_bytes=60000000),
        )(src_slot, src_cell, *inputs)
        keep = lambda v: pltpu.with_memory_space_constraint(v, pltpu.VMEM)
        return pl.pallas_call(
            finish,
            out_shape=jax.ShapeDtypeStruct(shape, BF16),
            in_specs=[vmem] * 4,
            out_specs=hbm,
            scratch_shapes=[pltpu.VMEM(shape[1:], BF16), dma((TICKS - 1 + PIECES,))],
            compiler_params=pltpu.CompilerParams(vmem_limit_bytes=16 * 1024 * 1024),
        )(keep(early), keep(mid), keep(mult), jnp.asarray(consts["ty"]))

    in_specs = (
        P(None, "gx", "gy", None),
        P(None, "gx", "gy", None),
        P("gx", "gy"),
        P(None, "gx", "gy"),
        P(),
        P("gx", "gy"),
        P("gx", "gy"),
        P(),
        P(),
    )
    out_specs = P(None, None, "gx", "gy", None)
    return jax.shard_map(local, mesh=mesh, in_specs=in_specs, out_specs=out_specs, check_vma=False)
```

profile of v0, /device:TPU:20, one launch (start us, length us, event | category | flops | bytes accessed | tf_op | source)
XLA Modules:
  0.0 24.9 jit_solution(5139595543292310981)
XLA Ops:
  0.0 0.0 copy-start
  2.0 21.2 %shard_map.217 = (bf16[2,2,32,64,128]{4,3,2,1,0:T(8,128)(2,1)S(1)}, f32[2,32,64,128]{3,2,1,0:T(8,128)S(1)}, f32[2,32,64,128]{3,2,1,0:T(8,128)S(1)}) custom-call(s32[1,1]{1,0:T(1,128)S(6)} %copy.24.refs_0_, s32[1,1]{1,0:T(1,128)S(6)} %copy.25.refs_1_, s32[1,4]{1,0:T(1,128)} %bitcast.5, f32[2,13]{1,0:T(2,128)} %refs_3_.1, f32[1,1]{1,0:T(1,128)} %bitcast.3.refs_4_, ...), custom_call_target="tpu_custom_call" | custom-call | tf_op jit(solution)/shard_map/pallas_call | solution.py:506
  23.1 0.0 copy-done
  23.1 1.7 %shard_map.218 = bf16[3,2,32,64,128]{4,3,2,1,0:T(8,128)(2,1)} custom-call(bf16[2,2,32,64,128]{4,3,2,1,0:T(8,128)(2,1)S(1)} %get-tuple-element.8.early, f32[2,32,64,128]{3,2,1,0:T(8,128)S(1)} %get-tuple-element.9.mid, f32[2,32,64,128]{3,2,1,0:T(8,128)S(1)} %get-tuple-element.10.mult, bf16[128,128]{1,0:T(8,128)(2,1)S(1)} %copy-done), custom_call_target="tpu_custom_call" | custom-call | tf_op jit(solution)/shard_map/pallas_call | solution.py:538
Async XLA Ops:
  0.0 23.1 %copy-start = (bf16[128,128]{1,0:T(8,128)(2,1)S(1)}, bf16[128,128]{1,0:T(8,128)(2,1)}, u32[]{:S(2)}) copy-start(bf16[128,128]{1,0:T(8,128)(2,1)} %constant.34.clone.refs_15_.ty) | copy-start | bytes 98308
where the time goes:
time: 25.1 us; the launch traced here: 24.9 us
  Pallas kernels  22.9 us (91%)
  between operations  1.97 us (8%)
    pallas_call x1, Pallas kernels, local(): pl.pallas_call(functools.partial(kernel, n_gx, n_gy), out_shape=(pltpu.VM...  21.2 us
    pallas_call x1, Pallas kernels, local(): pl.pallas_call(finish, out_shape=jax.ShapeDtypeStruct(shape, BF16), in_sp...  1.71 us

commit v1 on v0

--- a/solution.py
+++ b/solution.py
@@ -11,7 +11,6 @@
 DEPTH = 4
 TICKS = 3
 PIECES = 4
-INNER_PIECES = 3
 SUB = 8
 damping_ratio = 0.25
 absorb_peak = 4.0
@@ -45,18 +44,6 @@
     return np.concatenate([np.concatenate([high, high], 1), np.concatenate([low, np.zeros_like(low)], 1)], 0)
 
 
-def edges_first(table, depth):
-    rows = table.shape[0] // 2
-    cut = depth * SUB
-    return np.concatenate([table[:cut], table[rows:rows + cut], table[cut:rows], table[rows + cut:]], axis=0)
-
-
-def segments(sx):
-    inner = (sx - 2 * DEPTH) // INNER_PIECES
-    bounds = [(0, DEPTH), (sx - DEPTH, sx)]
-    return bounds + [(DEPTH + k * inner, DEPTH + (k + 1) * inner) for k in range(INNER_PIECES)]
-
-
 def split(values):
     high = values.astype(BF16).astype(F32)
     return high, values - high
@@ -97,23 +84,29 @@
     eye = np.eye(SUB)
     groups = sy // SUB
     ls = [np_split(np.kron(np.eye(sx), by[g * SUB:(g + 1) * SUB, :DEPTH])) for g in range(groups)]
-    lsh = np.stack([np.concatenate([h, h], axis=1) for h, _ in ls])
+    lsh = np.stack([h for h, _ in ls])
     lsl = np.stack([low for _, low in ls])
     half = sx // 2
     order = np.concatenate([np.arange(0, sx, 2), np.arange(1, sx, 2)])
     bxo, exo = bx[order], ex[order]
     lw = left3(np.kron(bxo[:, :DEPTH], eye))
     lw = np.concatenate([lw, np.zeros((lw.shape[0], 4 * SUB), lw.dtype)], axis=1)
+    even = np.kron(bx[:half, order[:half]], eye)
+    odd = np.kron(bx[:half, order[half:]], eye)
     zh, zl = np_split(bz)
     zz = np.concatenate([np.concatenate([zh, zl], 1)] * 2, 0)
     return dict(
         lsh=lsh.reshape(groups // 2, -1, lsh.shape[2]),
         lsl=lsl,
         lw=lw,
-        te=edges_first(fold(np.kron(bx[:half, order[:half]], eye)), DEPTH),
-        to=edges_first(fold(np.kron(bx[:half, order[half:]], eye)), DEPTH),
+        te=left3(even),
+        to=left3(odd),
+        tee=fold(even[:DEPTH * SUB]),
+        toe=fold(odd[:DEPTH * SUB]),
+        ln=np.stack([np.concatenate(np_split(np.kron(np.eye(half), by[sy - DEPTH:, g * SUB:(g + 1) * SUB])), axis=1) for g in range(groups)]),
+        tn=left3(np.kron(bxo.T, np.eye(DEPTH))),
         ts=left3(np.kron(bxo, np.eye(DEPTH))),
-        ty=fold(by),
+        ty=left3(by),
         zz=zz,
         bxr=np.repeat(bxo, SUB, axis=0).astype(np.float32),
         byf=by.astype(np.float32),
@@ -125,8 +118,8 @@
 
 
 SCALARS = ("pml", "amp", "wave")
-INVERSE_UNROLL = 2
-NAMES = ("lsh", "lsl", "lw", "te", "to", "ts", "ty", "zz", "bxr", "byf", "bzf", "exr", "eyr", "ezr")
+INVERSE_UNROLL = 8
+NAMES = ("lsh", "lsl", "lw", "te", "to", "tee", "toe", "ln", "tn", "ts", "ty", "zz", "bxr", "byf", "bzf", "exr", "eyr", "ezr")
 
 
 INPUTS = SCALARS + ("west_in", "south_in", "region", "vel") + NAMES
@@ -137,7 +130,7 @@
 def finish_plane(x, mid, mult, ty):
     sz = mid.shape[3]
     plane = jnp.concatenate([mid[0, x], mid[1, x]], axis=1)
-    raw = halves(mm(ty[...], right2(plane)))
+    raw = mm(ty[...], right3(plane))
     re, im = raw[:, :sz], raw[:, sz:]
     mr, mi = mult[0, x], mult[1, x]
     fr = re + mr * re - mi * im
@@ -167,14 +160,14 @@
 
 def kernel(n_gx, n_gy, *refs):
     slot, cell = refs[:2]
-    outside, (obuf, mid, mult), refs = refs[2:23], refs[23:26], refs[26:]
-    inside, refs = refs[:21], refs[21:]
+    outside, (obuf, mid, mult), refs = refs[2:27], refs[27:30], refs[30:]
+    inside, refs = refs[:25], refs[25:]
     pml, amp, wave = inside[:3]
     (west_in, south_in, region, vel,
-     lsh, lsl, lw0, te, to, ts, ty, zz, bxr, byf, bzf, exr, eyr, ezr) = inside[3:]
+     lsh, lsl, lw0, te, to, tee, toe, ln, tn, ts, ty, zz, bxr, byf, bzf, exr, eyr, ezr) = inside[3:]
     (
      west_buf, south_buf, east_buf, north_buf,
-     lw, point, pq, reg2, ab, rs, wf, sp,
+     lw, point, pq, reg2, ab, rs, wf, sp, nacc, mn,
      send_e, recv_w, send_n, recv_s, load_sem) = refs
     sx, sy = region.shape
     sz = vel.shape[1]
@@ -261,25 +254,44 @@
         portion = jnp.maximum(thick - distance, 0.0) / jnp.maximum(jnp.full_like(distance, thick), 1.0)
         return portion * portion
 
-    sigma = ramp(0, xi) + ramp(1, sx - 1.0 - xi) + ramp(2, yi) + ramp(3, sy - 1.0 - yi)
-    sigma = absorb_peak * sigma
-    den = diagonal_base * diagonal_base + sigma * sigma
-    ab[...] = jnp.where(lane2 < sy, diagonal_base, -sigma) / den
+    def coefficients(x, y, real):
+        sigma = ramp(0, x) + ramp(1, sx - 1.0 - x) + ramp(2, y) + ramp(3, sy - 1.0 - y)
+        sigma = absorb_peak * sigma
+        return jnp.where(real, diagonal_base, -sigma) / (diagonal_base * diagonal_base + sigma * sigma)
+
+    ab[...] = coefficients(xi, yi, lane2 < sy)
     reg2[...] = jnp.concatenate([region[...], region[...]], axis=1)
     ch, cl = split(vel[...] - w)
     contrast = jnp.concatenate([ch, ch, cl, cl], axis=0).astype(BF16)
     label = lax.broadcasted_iota(jnp.int32, (labels, 2 * sy), 0)
 
-    def mult_plane(x, carry):
-        own = jnp.where(reg2[pl.ds(x, 1), :] == label, ab[pl.ds(x, 1), :], 0.0)
+    def expand(own):
         oh, ol = split(own)
         lhs = jnp.concatenate([oh, ol, oh, ol], axis=0).astype(BF16)
-        res = lax.dot_general(lhs, contrast, (((0,), (0,)), ((), ())), preferred_element_type=F32)
+        return lax.dot_general(lhs, contrast, (((0,), (0,)), ((), ())), preferred_element_type=F32)
+
+    edge = sx * DEPTH
+    lane_n = lax.broadcasted_iota(jnp.int32, (labels, 2 * edge), 1)
+    place = lane_n % edge
+    north_ab = coefficients((place // DEPTH).astype(F32), (sy - DEPTH + place % DEPTH).astype(F32), lane_n < edge)
+    y_of = sy - DEPTH + lax.broadcasted_iota(jnp.int32, (sy, 2 * edge), 1) % DEPTH
+    pick = jnp.where(lax.broadcasted_iota(jnp.int32, (sy, 2 * edge), 0) == y_of, 1.0, 0.0).astype(BF16)
+    spread_out = mm(region[...].astype(F32).astype(BF16), pick)
+    x_of = (lax.broadcasted_iota(jnp.int32, (sx, 2 * edge), 1) % edge) // DEPTH
+    own_row = lax.broadcasted_iota(jnp.int32, (sx, 2 * edge), 0) == x_of
+    north_label = jnp.sum(jnp.where(own_row, spread_out, 0.0), axis=0, keepdims=True)
+    north_mult = expand(jnp.where(north_label == lax.broadcasted_iota(jnp.int32, (labels, 2 * edge), 0).astype(F32), north_ab, 0.0))
+    mn[0] = north_mult[:edge]
+    mn[1] = north_mult[edge:]
+
+    def mult_plane(x, carry):
+        res = expand(jnp.where(reg2[pl.ds(x, 1), :] == label, ab[pl.ds(x, 1), :], 0.0))
         mult[0, x] = res[:sy]
         mult[1, x] = res[sy:]
         return carry
 
-    lax.fori_loop(0, sx, mult_plane, 0, unroll=8)
+    for x in list(range(DEPTH)) + list(range(sx - DEPTH, sx)):
+        mult_plane(x, 0)
 
     @pl.when(jnp.logical_and(has_e, has_n))
     def _():
@@ -295,27 +307,37 @@
             send_sem=send_e.at[t, p], recv_sem=recv_w.at[t, p],
             device_id=(a + 1, b), device_id_type=MESH)
 
-    spans = segments(sx)
-
-    def north_copy(t, k):
-        rows = pl.ds(spans[k][0] * DEPTH, (spans[k][1] - spans[k][0]) * DEPTH)
+    def north_copy(t):
         return pltpu.make_async_remote_copy(
-            src_ref=north_buf.at[t, :, rows, :], dst_ref=south_buf.at[t, :, rows, :],
-            send_sem=send_n.at[t, k], recv_sem=recv_s.at[t, k],
+            src_ref=north_buf.at[t], dst_ref=south_buf.at[t],
+            send_sem=send_n.at[t], recv_sem=recv_s.at[t],
             device_id=(a, b + 1), device_id_type=MESH)
 
     def spread(q, even_in, odd_in, low, high):
-        whole = low == 0 and high == sx // 2
-
-        def planes(table, values):
-            if not whole:
-                return halves(mm(table[2 * low * SUB:2 * high * SUB, :], values))
-            out = mm(table[...], values)
-            edge = 2 * DEPTH * SUB
-            return jnp.concatenate([halves(out[:edge]), halves(out[edge:])], axis=0)
-
-        even = planes(te, even_in)
-        odd = planes(to, odd_in)
+        if high == DEPTH:
+            cut = 2 * DEPTH * SUB
+            outs = []
+            for table, values, side in ((tee, even_in, 0), (toe, odd_in, 1)):
+                total = None
+                ends = []
+                for k in range(2):
+                    high_part, low_part = ln[2 * q + k, :, :span // 2], ln[2 * q + k, :, span // 2:]
+                    lhs = jnp.concatenate([
+                        table[...],
+                        jnp.concatenate([high_part, high_part], axis=1),
+                        jnp.concatenate([low_part, jnp.zeros_like(low_part)], axis=1)], axis=0)
+                    out = mm(lhs, values[:, 2 * k * sz:2 * (k + 1) * sz])
+                    ends.append(halves(out[:cut]))
+                    part = halves(out[cut:])
+                    total = part if total is None else total + part
+                rows = pl.ds(side * edge // 2, edge // 2)
+                nacc[rows, :] = total if q == 0 else nacc[rows, :] + total
+                outs.append(jnp.concatenate(ends, axis=1))
+            even, odd = outs
+        else:
+            rows = slice(low * SUB, high * SUB)
+            even = mm(te[rows, :], jnp.concatenate([even_in, even_in[:span // 2]], axis=0))
+            odd = mm(to[rows, :], jnp.concatenate([odd_in, odd_in[:span // 2]], axis=0))
         res = jnp.concatenate([even + odd, even - odd], axis=0)
         size = res.shape[0]
         done = along_z(jnp.concatenate([res[:, n * sz:(n + 1) * sz] for n in range(4)], axis=0), zz[...])
@@ -331,65 +353,44 @@
 
     need("west_in", "south_in", "ty", "zz", "ts")
     zpad = jnp.zeros((SUB, sz), F32)
-    row8 = lax.broadcasted_iota(jnp.int32, (SUB, sz), 0)
 
     for t in range(TICKS):
         west = west_in if t == 0 else west_buf.at[t - 1]
         south = south_in if t == 0 else south_buf.at[t - 1]
-        def take_west(p):
+        def take_west():
             if t > 0:
                 @pl.when(has_w)
                 def _():
-                    east_copy(t - 1, p).wait_recv()
+                    for p in range(DEPTH // 2):
+                        east_copy(t - 1, p).wait_recv()
 
             planes = []
-            for j in range(2 * p, 2 * p + 2):
+            for j in range(DEPTH):
                 plane = jnp.concatenate([west[0, j], west[1, j]], axis=1)
-                planes.append(halves(mm(ty[...], right2(plane))))
+                planes.append(mm(ty[...], right3(plane)))
             rows = [q[:, c * sz:(c + 1) * sz] for c in range(2) for q in planes]
             done = along_z(jnp.concatenate(rows, axis=0), zz[...])
-            wf[:, 2 * p:2 * p + 2] = done.reshape(2, 2, sy, sz)
-
-        def take_south(parts):
-            if t > 0:
-                @pl.when(has_s)
-                def _():
-                    for k in parts:
-                        north_copy(t - 1, k).wait_recv()
-
-            cuts = [slice(spans[k][0] * DEPTH, spans[k][1] * DEPTH) for k in parts]
-            done = along_z(jnp.concatenate([south[c, rows, :] for c in range(2) for rows in cuts], axis=0), zz[...])
-            size = done.shape[0] // 2
-            both = jnp.concatenate([done[:size], done[size:]], axis=1)
-            at = 0
-            for k, rows in zip(parts, cuts):
-                step = rows.stop - rows.start
-                arrived[k] = both[at:at + step]
-                at += step
-
-        arrived = {}
-        every = list(range(len(spans)))
-        take_west(0)
+            wf[...] = done.reshape(2, DEPTH, sy, sz)
+
+        if t > 0:
+            @pl.when(has_s)
+            def _():
+                north_copy(t - 1).wait_recv()
+
+        done = along_z(jnp.concatenate([south[0], south[1]], axis=0), zz[...])
+        done = jnp.concatenate([done[:edge], done[edge:]], axis=1)
+        rs[...] = right2(mm(ts[...], right3(done)))
+        take_west()
+
         if t == 0:
-            take_south(every)
-            take_west(1)
-        else:
-            take_west(1)
-            take_south(every[:2])
-            for k in every[2:]:
-                take_south([k])
-        in_order = sorted(every, key=lambda k: spans[k][0])
-        rs[...] = right2(mm(ts[...], right3(jnp.concatenate([arrived[k] for k in in_order], axis=0))))
-
-        if t == 0:
-            need("lsh", "lsl", "te", "to", "amp")
+            need("lsh", "lsl", "te", "to", "tee", "toe", "ln", "tn", "amp")
 
         source = t - a - b + (n_gx + n_gy - 2)
         live = jnp.where(slot[0, 0] == source, 1.0, 0.0).astype(F32)
         amps = (amp[0, source] * live, amp[1, source] * live)
 
         def spectrum(q):
-            shared = mm(lsh[q], rs[...])
+            shared = mm(jnp.concatenate([lsh[q], lsh[q]], axis=1), rs[...])
             specs = []
             for k in range(2):
                 g = 2 * q + k
@@ -401,8 +402,7 @@
                     ph, pw = split(p * amps[c])
                     parts.append(jnp.concatenate([wh, wl, wh, ph, pw, ph, zpad], axis=0).astype(BF16))
                 rw = jnp.concatenate([rs[: sx * DEPTH, :], jnp.concatenate(parts, axis=1)], axis=0)
-                lhs = jnp.concatenate([lsl[g], lw[...]], axis=1)
-                coeffs = shared[k * span:(k + 1) * span] + mm(lhs, rw)
+                coeffs = shared[k * span:(k + 1) * span] + mm(jnp.concatenate([lsl[g], lw[...]], axis=1), rw)
                 c0, c1 = coeffs[:, :sz], coeffs[:, sz:]
                 pr, qr = pq[0, g], pq[1, g]
                 specs += [c0 * pr + c1 * qr, c1 * pr - c0 * qr]
@@ -430,43 +430,36 @@
             obuf[t, 1, x] = fi.astype(BF16)
             return fr, fi
 
-        def two_planes(i, east):
-            first = one_plane(2 * i)
-            second = one_plane(2 * i + 1)
-            if t + 1 < TICKS:
-                rows = pl.ds(pl.multiple_of(i * SUB, SUB), SUB)
+        def east_planes(p):
+            for j in range(2 * p, 2 * p + 2):
+                field = one_plane(sx - DEPTH + j)
                 for c in range(2):
-                    one = pltpu.roll(first[c][sy - SUB:], DEPTH, 0)
-                    north_buf[t, c, rows, :] = jnp.where(row8 < DEPTH, one, second[c][sy - SUB:])
-                    if east is not None:
-                        east_buf[t, c, 2 * i - (sx - DEPTH)] = first[c]
-                        east_buf[t, c, 2 * i + 1 - (sx - DEPTH)] = second[c]
-
-        for i in range((sx - DEPTH) // 2, sx // 2):
-            two_planes(i, True)
+                    east_buf[t, c, j] = field[c]
 
             @pl.when(has_e)
             def _():
-                east_copy(t, i - (sx - DEPTH) // 2).start()
-
-        for i in range(DEPTH // 2):
-            two_planes(i, None)
+                east_copy(t, p).start()
+
+        back = mm(tn[...], right3(nacc[...]))
+        back = along_z(jnp.concatenate([back[:, :sz], back[:, sz:]], axis=0), zz[...])
+        east_planes(0)
+        re, im = back[:edge], back[edge:]
+        north_buf[t, 0] = re + mn[0] * re - mn[1] * im
+        north_buf[t, 1] = im + mn[0] * im + mn[1] * re
+        east_planes(1)
 
         @pl.when(has_n)
         def _():
-            north_copy(t, 0).start()
-            north_copy(t, 1).start()
+            north_copy(t).start()
+
+        if t == 0:
+            lax.fori_loop(DEPTH, sx - DEPTH, mult_plane, 0, unroll=8)
 
         for q in range(groups // 2):
             spread(q, sp[2 * q], sp[2 * q + 1], DEPTH, sx // 2)
 
-        for k in range(2, len(spans)):
-            for i in range(spans[k][0] // 2, spans[k][1] // 2):
-                two_planes(i, None)
-
-            @pl.when(has_n)
-            def _():
-                north_copy(t, k).start()
+        for x in range(sx - DEPTH):
+            one_plane(x)
 
     for t in range(TICKS - 1):
         if t + 1 < TICKS:
@@ -477,8 +470,7 @@
 
             @pl.when(has_n)
             def _():
-                for k in range(len(spans)):
-                    north_copy(t, k).wait_send()
+                north_copy(t).wait_send()
 
 
 def solution(mesh):
@@ -525,10 +517,12 @@
                 pltpu.VMEM((2 * sx * DEPTH, 2 * sz), BF16),
                 pltpu.VMEM((2, DEPTH, sy, sz), F32),
                 pltpu.VMEM((groups, sx * SUB, 4 * sz), BF16),
+                pltpu.VMEM((sx * DEPTH, 2 * sz), F32),
+                pltpu.VMEM((2, sx * DEPTH, sz), F32),
                 dma((TICKS - 1, DEPTH // 2)),
                 dma((TICKS - 1, DEPTH // 2)),
-                dma((TICKS - 1, INNER_PIECES + 2)),
-                dma((TICKS - 1, INNER_PIECES + 2)),
+                dma((TICKS - 1,)),
+                dma((TICKS - 1,)),
                 dma((len(inputs),)),
             ],
             compiler_params=pltpu.CompilerParams(

time: 25.1 us -> 22.7 us (0.904)
  Pallas kernels: 22.9 us -> 20.5 us
    pallas_call x1, Pallas kernels: 21.2 us -> 18.8 us  [local(): pl.pallas_call(functools.partial(kernel, n_gx, n_gy), out_shape=(pltpu.VM...]
where the time goes in v1:
time: 22.7 us; the launch traced here: 22.5 us
  Pallas kernels  20.5 us (90%)
  between operations  1.97 us (9%)
    pallas_call x1, Pallas kernels, local(): pl.pallas_call(functools.partial(kernel, n_gx, n_gy), out_shape=(pltpu.VM...  18.8 us
    pallas_call x1, Pallas kernels, local(): pl.pallas_call(finish, out_shape=jax.ShapeDtypeStruct(shape, BF16), in_sp...  1.71 us

profile of v1, /device:TPU:20, one launch (start us, length us, event | category | flops | bytes accessed | tf_op | source)
XLA Modules:
  0.0 22.5 jit_solution(10243384863903786805)
XLA Ops:
  0.0 0.0 copy-start
  2.0 18.8 %shard_map.253 = (bf16[2,2,32,64,128]{4,3,2,1,0:T(8,128)(2,1)S(1)}, f32[2,32,64,128]{3,2,1,0:T(8,128)S(1)}, f32[2,32,64,128]{3,2,1,0:T(8,128)S(1)}) custom-call(s32[1,1]{1,0:T(1,128)S(6)} %copy.28.refs_0_, s32[1,1]{1,0:T(1,128)S(6)} %copy.29.refs_1_, s32[1,4]{1,0:T(1,128)} %bitcast.5, f32[2,13]{1,0:T(2,128)} %refs_3_.1, f32[1,1]{1,0:T(1,128)} %bitcast.3.refs_4_, ...), custom_call_target="tpu_custom_call" | custom-call | tf_op jit(solution)/shard_map/pallas_call | solution.py:498
  20.8 0.0 copy-done
  20.8 1.7 %shard_map.254 = bf16[3,2,32,64,128]{4,3,2,1,0:T(8,128)(2,1)} custom-call(bf16[2,2,32,64,128]{4,3,2,1,0:T(8,128)(2,1)S(1)} %get-tuple-element.8.early, f32[2,32,64,128]{3,2,1,0:T(8,128)S(1)} %get-tuple-element.9.mid, f32[2,32,64,128]{3,2,1,0:T(8,128)S(1)} %get-tuple-element.10.mult, bf16[64,192]{1,0:T(8,128)(2,1)S(1)} %copy-done), custom_call_target="tpu_custom_call" | custom-call | tf_op jit(solution)/shard_map/pallas_call | solution.py:532
Async XLA Ops:
  0.0 20.8 %copy-start = (bf16[64,192]{1,0:T(8,128)(2,1)S(1)}, bf16[64,192]{1,0:T(8,128)(2,1)}, u32[]{:S(2)}) copy-start(bf16[64,192]{1,0:T(8,128)(2,1)} %constant.46.clone.refs_19_.ty) | copy-start | bytes 73732

commit v2 on v1

--- a/solution.py
+++ b/solution.py
@@ -10,7 +10,7 @@
 
 DEPTH = 4
 TICKS = 3
-PIECES = 4
+PIECES = 8
 SUB = 8
 damping_ratio = 0.25
 absorb_peak = 4.0
@@ -123,7 +123,7 @@
 
 
 INPUTS = SCALARS + ("west_in", "south_in", "region", "vel") + NAMES
-FIRST = ("wave", "ezr", "eyr", "exr", "bxr", "byf", "bzf", "lw", "pml", "region", "vel")
+FIRST = ("wave", "ezr", "eyr", "exr", "bxr", "byf", "bzf", "lw", "pml", "region", "vel", "west_in", "south_in", "ty", "zz", "ts")
 ORDER = FIRST + tuple(name for name in INPUTS if name not in FIRST)
 
 
@@ -133,8 +133,8 @@
     raw = mm(ty[...], right3(plane))
     re, im = raw[:, :sz], raw[:, sz:]
     mr, mi = mult[0, x], mult[1, x]
-    fr = re + mr * re - mi * im
-    fi = im + mr * im + mi * re
+    fr = mr * re - mi * im
+    fi = mr * im + mi * re
     return fr, fi
 
 
@@ -207,7 +207,7 @@
     def _():
         south_buf[...] = jnp.zeros_like(south_buf)
 
-    need("wave", "exr", "eyr", "ezr")
+    need("wave", "exr", "eyr", "ezr", "bxr", "byf", "bzf", "lw", "pml", "region", "vel", "west_in", "south_in", "ty", "zz", "ts")
     w = wave[0, 0]
     damp = -damping_ratio * w
 
@@ -221,7 +221,6 @@
         return carry
 
     lax.fori_loop(0, groups, inverse_group, 0, unroll=INVERSE_UNROLL)
-    need("bxr", "byf", "bzf", "lw")
 
     position = cell[0, 0]
     px = position // (sy * sz)
@@ -247,8 +246,6 @@
     lane2 = lax.broadcasted_iota(jnp.int32, (sx, 2 * sy), 1)
     yi = (lane2 % sy).astype(F32)
 
-    need("pml", "region", "vel")
-
     def ramp(i, distance):
         thick = pml[0, i].astype(F32)
         portion = jnp.maximum(thick - distance, 0.0) / jnp.maximum(jnp.full_like(distance, thick), 1.0)
@@ -281,25 +278,17 @@
     own_row = lax.broadcasted_iota(jnp.int32, (sx, 2 * edge), 0) == x_of
     north_label = jnp.sum(jnp.where(own_row, spread_out, 0.0), axis=0, keepdims=True)
     north_mult = expand(jnp.where(north_label == lax.broadcasted_iota(jnp.int32, (labels, 2 * edge), 0).astype(F32), north_ab, 0.0))
-    mn[0] = north_mult[:edge]
+    mn[0] = 1.0 + north_mult[:edge]
     mn[1] = north_mult[edge:]
 
     def mult_plane(x, carry):
         res = expand(jnp.where(reg2[pl.ds(x, 1), :] == label, ab[pl.ds(x, 1), :], 0.0))
-        mult[0, x] = res[:sy]
+        mult[0, x] = 1.0 + res[:sy]
         mult[1, x] = res[sy:]
         return carry
 
     for x in list(range(DEPTH)) + list(range(sx - DEPTH, sx)):
         mult_plane(x, 0)
-
-    @pl.when(jnp.logical_and(has_e, has_n))
-    def _():
-        pl.semaphore_wait(barrier, 2)
-
-    @pl.when(jnp.logical_xor(has_e, has_n))
-    def _():
-        pl.semaphore_wait(barrier, 1)
 
     def east_copy(t, p):
         return pltpu.make_async_remote_copy(
@@ -351,7 +340,6 @@
                 for i in range(count):
                     mid[c, sx - 1 - low - i, rows, :] = block[count + i]
 
-    need("west_in", "south_in", "ty", "zz", "ts")
     zpad = jnp.zeros((SUB, sz), F32)
 
     for t in range(TICKS):
@@ -409,20 +397,20 @@
             spec = jnp.concatenate(specs, axis=1)
             return right2(spec[: span // 2]), right2(spec[span // 2:])
 
-        ahead = spectrum(0)
+        if t + 1 == TICKS:
+            ahead = spectrum(0)
+            for q in range(groups // 2):
+                even_in, odd_in = ahead
+                if q + 1 < groups // 2:
+                    ahead = spectrum(q + 1)
+                spread(q, even_in, odd_in, 0, sx // 2)
+            break
+
         for q in range(groups // 2):
-            even_in, odd_in = ahead
-            if q + 1 < groups // 2:
-                ahead = spectrum(q + 1)
-            if t + 1 == TICKS:
-                spread(q, even_in, odd_in, 0, sx // 2)
-            else:
-                sp[2 * q] = even_in
-                sp[2 * q + 1] = odd_in
-                spread(q, even_in, odd_in, 0, DEPTH)
-
-        if t + 1 == TICKS:
-            break
+            sp[2 * q], sp[2 * q + 1] = spectrum(q)
+        for q in range(groups // 2):
+            spread(q, sp[2 * q], sp[2 * q + 1], 0, DEPTH)
+
 
         def one_plane(x):
             fr, fi = finish_plane(x, mid, mult, ty)
@@ -440,12 +428,21 @@
             def _():
                 east_copy(t, p).start()
 
+        if t == 0:
+            @pl.when(jnp.logical_and(has_e, has_n))
+            def _():
+                pl.semaphore_wait(barrier, 2)
+
+            @pl.when(jnp.logical_xor(has_e, has_n))
+            def _():
+                pl.semaphore_wait(barrier, 1)
+
         back = mm(tn[...], right3(nacc[...]))
         back = along_z(jnp.concatenate([back[:, :sz], back[:, sz:]], axis=0), zz[...])
         east_planes(0)
         re, im = back[:edge], back[edge:]
-        north_buf[t, 0] = re + mn[0] * re - mn[1] * im
-        north_buf[t, 1] = im + mn[0] * im + mn[1] * re
+        north_buf[t, 0] = mn[0] * re - mn[1] * im
+        north_buf[t, 1] = mn[0] * im + mn[1] * re
         east_planes(1)
 
         @pl.when(has_n)

time: 22.7 us -> 22.5 us (level)
    pallas_call x1, Pallas kernels: 18.8 us -> 18.6 us  [local(): pl.pallas_call(functools.partial(kernel, n_gx, n_gy), out_shape=(pltpu.VM...]
where the time goes in v2:
time: 22.5 us; the launch traced here: 22.3 us
  Pallas kernels  20.3 us (90%)
  between operations  1.97 us (9%)
    pallas_call x1, Pallas kernels, local(): pl.pallas_call(functools.partial(kernel, n_gx, n_gy), out_shape=(pltpu.VM...  18.6 us
    pallas_call x1, Pallas kernels, local(): pl.pallas_call(finish, out_shape=jax.ShapeDtypeStruct(shape, BF16), in_sp...  1.74 us

profile of v2, /device:TPU:20, one launch (start us, length us, event | category | flops | bytes accessed | tf_op | source)
XLA Modules:
  0.0 22.3 jit_solution(389586680770885050)
XLA Ops:
  0.0 0.0 copy-start
  2.0 18.6 %shard_map.253 = (bf16[2,2,32,64,128]{4,3,2,1,0:T(8,128)(2,1)S(1)}, f32[2,32,64,128]{3,2,1,0:T(8,128)S(1)}, f32[2,32,64,128]{3,2,1,0:T(8,128)S(1)}) custom-call(s32[1,1]{1,0:T(1,128)S(6)} %copy.28.refs_0_, s32[1,1]{1,0:T(1,128)S(6)} %copy.29.refs_1_, s32[1,4]{1,0:T(1,128)} %bitcast.5, f32[2,13]{1,0:T(2,128)} %refs_3_.1, f32[1,1]{1,0:T(1,128)} %bitcast.3.refs_4_, ...), custom_call_target="tpu_custom_call" | custom-call | tf_op jit(solution)/shard_map/pallas_call | solution.py:495
  20.5 0.0 copy-done
  20.5 1.7 %shard_map.254 = bf16[3,2,32,64,128]{4,3,2,1,0:T(8,128)(2,1)} custom-call(bf16[2,2,32,64,128]{4,3,2,1,0:T(8,128)(2,1)S(1)} %get-tuple-element.8.early, f32[2,32,64,128]{3,2,1,0:T(8,128)S(1)} %get-tuple-element.9.mid, f32[2,32,64,128]{3,2,1,0:T(8,128)S(1)} %get-tuple-element.10.mult, bf16[64,192]{1,0:T(8,128)(2,1)S(1)} %copy-done), custom_call_target="tpu_custom_call" | custom-call | tf_op jit(solution)/shard_map/pallas_call | solution.py:529
Async XLA Ops:
  0.0 20.5 %copy-start = (bf16[64,192]{1,0:T(8,128)(2,1)S(1)}, bf16[64,192]{1,0:T(8,128)(2,1)}, u32[]{:S(2)}) copy-start(bf16[64,192]{1,0:T(8,128)(2,1)} %constant.46.clone.refs_19_.ty) | copy-start | bytes 73732

commit v3 on v2

--- a/solution.py
+++ b/solution.py
@@ -10,7 +10,7 @@
 
 DEPTH = 4
 TICKS = 3
-PIECES = 8
+PIECES = 4
 SUB = 8
 damping_ratio = 0.25
 absorb_peak = 4.0
@@ -141,7 +141,7 @@
 def finish(early, mid, mult, ty, out, last, sems):
     sx = mid.shape[1]
     count = early.shape[0]
-    copies = [pltpu.make_async_copy(early.at[t], out.at[t], sems.at[t]) for t in range(count)]
+    copies = [pltpu.make_async_copy(early, out.at[pl.ds(0, count)], sems.at[0])]
     for copy in copies:
         copy.start()
     size = sx // PIECES
@@ -167,7 +167,7 @@
      lsh, lsl, lw0, te, to, tee, toe, ln, tn, ts, ty, zz, bxr, byf, bzf, exr, eyr, ezr) = inside[3:]
     (
      west_buf, south_buf, east_buf, north_buf,
-     lw, point, pq, reg2, ab, rs, wf, sp, nacc, mn,
+     lw, point, pq, reg2, ab, rs, wf, sp, nacc, mn, west_side,
      send_e, recv_w, send_n, recv_s, load_sem) = refs
     sx, sy = region.shape
     sz = vel.shape[1]
@@ -327,18 +327,26 @@
             rows = slice(low * SUB, high * SUB)
             even = mm(te[rows, :], jnp.concatenate([even_in, even_in[:span // 2]], axis=0))
             odd = mm(to[rows, :], jnp.concatenate([odd_in, odd_in[:span // 2]], axis=0))
-        res = jnp.concatenate([even + odd, even - odd], axis=0)
+        mirror = list(range(sx - 1 - low, sx - 1 - high, -1))
+        if high == DEPTH:
+            west_side[q] = even + odd
+            res = even - odd
+            held = mirror
+        elif low == DEPTH:
+            res = jnp.concatenate([west_side[q], even + odd, even - odd], axis=0)
+            held = list(range(high)) + mirror
+        else:
+            res = jnp.concatenate([even + odd, even - odd], axis=0)
+            held = list(range(high)) + mirror
         size = res.shape[0]
         done = along_z(jnp.concatenate([res[:, n * sz:(n + 1) * sz] for n in range(4)], axis=0), zz[...])
-        count = high - low
         for k in range(2):
             rows = pl.ds((2 * q + k) * SUB, SUB)
             for c in range(2):
                 n = 2 * k + c
-                block = done[n * size:(n + 1) * size].reshape(2 * count, SUB, sz)
-                mid[c, low:high, rows, :] = block[:count]
-                for i in range(count):
-                    mid[c, sx - 1 - low - i, rows, :] = block[count + i]
+                block = done[n * size:(n + 1) * size].reshape(len(held), SUB, sz)
+                for i, x in enumerate(held):
+                    mid[c, x, rows, :] = block[i]
 
     zpad = jnp.zeros((SUB, sz), F32)
 
@@ -346,12 +354,6 @@
         west = west_in if t == 0 else west_buf.at[t - 1]
         south = south_in if t == 0 else south_buf.at[t - 1]
         def take_west():
-            if t > 0:
-                @pl.when(has_w)
-                def _():
-                    for p in range(DEPTH // 2):
-                        east_copy(t - 1, p).wait_recv()
-
             planes = []
             for j in range(DEPTH):
                 plane = jnp.concatenate([west[0, j], west[1, j]], axis=1)
@@ -364,6 +366,11 @@
             @pl.when(has_s)
             def _():
                 north_copy(t - 1).wait_recv()
+
+            @pl.when(has_w)
+            def _():
+                for p in range(DEPTH // 2):
+                    east_copy(t - 1, p).wait_recv()
 
         done = along_z(jnp.concatenate([south[0], south[1]], axis=0), zz[...])
         done = jnp.concatenate([done[:edge], done[edge:]], axis=1)
@@ -437,9 +444,9 @@
             def _():
                 pl.semaphore_wait(barrier, 1)
 
+        east_planes(0)
         back = mm(tn[...], right3(nacc[...]))
         back = along_z(jnp.concatenate([back[:, :sz], back[:, sz:]], axis=0), zz[...])
-        east_planes(0)
         re, im = back[:edge], back[edge:]
         north_buf[t, 0] = mn[0] * re - mn[1] * im
         north_buf[t, 1] = mn[0] * im + mn[1] * re
@@ -516,6 +523,7 @@
                 pltpu.VMEM((groups, sx * SUB, 4 * sz), BF16),
                 pltpu.VMEM((sx * DEPTH, 2 * sz), F32),
                 pltpu.VMEM((2, sx * DEPTH, sz), F32),
+                pltpu.VMEM((groups // 2, DEPTH * SUB, 4 * sz), F32),
                 dma((TICKS - 1, DEPTH // 2)),
                 dma((TICKS - 1, DEPTH // 2)),
                 dma((TICKS - 1,)),

time: 22.5 us -> 22.3 us (level)
  no operation moved by 1% of the time
where the time goes in v3:
time: 22.3 us; the launch traced here: 22.1 us
  Pallas kernels  20.1 us (90%)
  between operations  1.97 us (9%)
    pallas_call x1, Pallas kernels, local(): pl.pallas_call(functools.partial(kernel, n_gx, n_gy), out_shape=(pltpu.VM...  18.4 us
    pallas_call x1, Pallas kernels, local(): pl.pallas_call(finish, out_shape=jax.ShapeDtypeStruct(shape, BF16), in_sp...  1.71 us

profile of v3, /device:TPU:20, one launch (start us, length us, event | category | flops | bytes accessed | tf_op | source)
XLA Modules:
  0.0 22.1 jit_solution(10672893650808696740)
XLA Ops:
  0.0 0.0 copy-start
  2.0 18.4 %shard_map.253 = (bf16[2,2,32,64,128]{4,3,2,1,0:T(8,128)(2,1)S(1)}, f32[2,32,64,128]{3,2,1,0:T(8,128)S(1)}, f32[2,32,64,128]{3,2,1,0:T(8,128)S(1)}) custom-call(s32[1,1]{1,0:T(1,128)S(6)} %copy.28.refs_0_, s32[1,1]{1,0:T(1,128)S(6)} %copy.29.refs_1_, s32[1,4]{1,0:T(1,128)} %bitcast.5, f32[2,13]{1,0:T(2,128)} %refs_3_.1, f32[1,1]{1,0:T(1,128)} %bitcast.3.refs_4_, ...), custom_call_target="tpu_custom_call" | custom-call | tf_op jit(solution)/shard_map/pallas_call | solution.py:502
  20.4 0.0 copy-done
  20.4 1.7 %shard_map.254 = bf16[3,2,32,64,128]{4,3,2,1,0:T(8,128)(2,1)} custom-call(bf16[2,2,32,64,128]{4,3,2,1,0:T(8,128)(2,1)S(1)} %get-tuple-element.8.early, f32[2,32,64,128]{3,2,1,0:T(8,128)S(1)} %get-tuple-element.9.mid, f32[2,32,64,128]{3,2,1,0:T(8,128)S(1)} %get-tuple-element.10.mult, bf16[64,192]{1,0:T(8,128)(2,1)S(1)} %copy-done), custom_call_target="tpu_custom_call" | custom-call | tf_op jit(solution)/shard_map/pallas_call | solution.py:537
Async XLA Ops:
  0.0 20.4 %copy-start = (bf16[64,192]{1,0:T(8,128)(2,1)S(1)}, bf16[64,192]{1,0:T(8,128)(2,1)}, u32[]{:S(2)}) copy-start(bf16[64,192]{1,0:T(8,128)(2,1)} %constant.46.clone.refs_19_.ty) | copy-start | bytes 73732

commit v4 on v3

--- a/solution.py
+++ b/solution.py
@@ -287,7 +287,7 @@
         mult[1, x] = res[sy:]
         return carry
 
-    for x in list(range(DEPTH)) + list(range(sx - DEPTH, sx)):
+    for x in range(sx - DEPTH, sx):
         mult_plane(x, 0)
 
     def east_copy(t, p):
@@ -457,7 +457,8 @@
             north_copy(t).start()
 
         if t == 0:
-            lax.fori_loop(DEPTH, sx - DEPTH, mult_plane, 0, unroll=8)
+            for x in range(sx - DEPTH):
+                mult_plane(x, 0)
 
         for q in range(groups // 2):
             spread(q, sp[2 * q], sp[2 * q + 1], DEPTH, sx // 2)

time: 22.3 us -> 22.3 us (level)
  no operation moved by 1% of the time
where the time goes in v4:
time: 22.3 us; the launch traced here: 22.1 us
  Pallas kernels  20.1 us (90%)
  between operations  1.97 us (9%)
    pallas_call x1, Pallas kernels, local(): pl.pallas_call(functools.partial(kernel, n_gx, n_gy), out_shape=(pltpu.VM...  18.4 us
    pallas_call x1, Pallas kernels, local(): pl.pallas_call(finish, out_shape=jax.ShapeDtypeStruct(shape, BF16), in_sp...  1.71 us

profile of v4, /device:TPU:20, one launch (start us, length us, event | category | flops | bytes accessed | tf_op | source)
XLA Modules:
  0.0 22.1 jit_solution(11613437089334838043)
XLA Ops:
  0.0 0.0 copy-start
  2.0 18.4 %shard_map.253 = (bf16[2,2,32,64,128]{4,3,2,1,0:T(8,128)(2,1)S(1)}, f32[2,32,64,128]{3,2,1,0:T(8,128)S(1)}, f32[2,32,64,128]{3,2,1,0:T(8,128)S(1)}) custom-call(s32[1,1]{1,0:T(1,128)S(6)} %copy.28.refs_0_, s32[1,1]{1,0:T(1,128)S(6)} %copy.29.refs_1_, s32[1,4]{1,0:T(1,128)} %bitcast.5, f32[2,13]{1,0:T(2,128)} %refs_3_.1, f32[1,1]{1,0:T(1,128)} %bitcast.3.refs_4_, ...), custom_call_target="tpu_custom_call" | custom-call | tf_op jit(solution)/shard_map/pallas_call | solution.py:503
  20.4 0.0 copy-done
  20.4 1.7 %shard_map.254 = bf16[3,2,32,64,128]{4,3,2,1,0:T(8,128)(2,1)} custom-call(bf16[2,2,32,64,128]{4,3,2,1,0:T(8,128)(2,1)S(1)} %get-tuple-element.8.early, f32[2,32,64,128]{3,2,1,0:T(8,128)S(1)} %get-tuple-element.9.mid, f32[2,32,64,128]{3,2,1,0:T(8,128)S(1)} %get-tuple-element.10.mult, bf16[64,192]{1,0:T(8,128)(2,1)S(1)} %copy-done), custom_call_target="tpu_custom_call" | custom-call | tf_op jit(solution)/shard_map/pallas_call | solution.py:538
Async XLA Ops:
  0.0 20.4 %copy-start = (bf16[64,192]{1,0:T(8,128)(2,1)S(1)}, bf16[64,192]{1,0:T(8,128)(2,1)}, u32[]{:S(2)}) copy-start(bf16[64,192]{1,0:T(8,128)(2,1)} %constant.46.clone.refs_19_.ty) | copy-start | bytes 73732

commit v5 on v4

--- a/solution.py
+++ b/solution.py
@@ -10,7 +10,7 @@
 
 DEPTH = 4
 TICKS = 3
-PIECES = 4
+PIECES = 2
 SUB = 8
 damping_ratio = 0.25
 absorb_peak = 4.0

time: 22.3 us -> 22.3 us (level)
  no operation moved by 1% of the time
where the time goes in v5:
time: 22.3 us; the launch traced here: 22.1 us
  Pallas kernels  20.1 us (90%)
  between operations  1.97 us (9%)
    pallas_call x1, Pallas kernels, local(): pl.pallas_call(functools.partial(kernel, n_gx, n_gy), out_shape=(pltpu.VM...  18.4 us
    pallas_call x1, Pallas kernels, local(): pl.pallas_call(finish, out_shape=jax.ShapeDtypeStruct(shape, BF16), in_sp...  1.69 us

profile of v5, /device:TPU:20, one launch (start us, length us, event | category | flops | bytes accessed | tf_op | source)
XLA Modules:
  0.0 22.1 jit_solution(7837060088854730988)
XLA Ops:
  0.0 0.0 copy-start
  2.0 18.4 %shard_map.253 = (bf16[2,2,32,64,128]{4,3,2,1,0:T(8,128)(2,1)S(1)}, f32[2,32,64,128]{3,2,1,0:T(8,128)S(1)}, f32[2,32,64,128]{3,2,1,0:T(8,128)S(1)}) custom-call(s32[1,1]{1,0:T(1,128)S(6)} %copy.28.refs_0_, s32[1,1]{1,0:T(1,128)S(6)} %copy.29.refs_1_, s32[1,4]{1,0:T(1,128)} %bitcast.5, f32[2,13]{1,0:T(2,128)} %refs_3_.1, f32[1,1]{1,0:T(1,128)} %bitcast.3.refs_4_, ...), custom_call_target="tpu_custom_call" | custom-call | tf_op jit(solution)/shard_map/pallas_call | solution.py:503
  20.4 0.0 copy-done
  20.4 1.7 %shard_map.254 = bf16[3,2,32,64,128]{4,3,2,1,0:T(8,128)(2,1)} custom-call(bf16[2,2,32,64,128]{4,3,2,1,0:T(8,128)(2,1)S(1)} %get-tuple-element.8.early, f32[2,32,64,128]{3,2,1,0:T(8,128)S(1)} %get-tuple-element.9.mid, f32[2,32,64,128]{3,2,1,0:T(8,128)S(1)} %get-tuple-element.10.mult, bf16[64,192]{1,0:T(8,128)(2,1)S(1)} %copy-done), custom_call_target="tpu_custom_call" | custom-call | tf_op jit(solution)/shard_map/pallas_call | solution.py:538
Async XLA Ops:
  0.0 20.4 %copy-start = (bf16[64,192]{1,0:T(8,128)(2,1)S(1)}, bf16[64,192]{1,0:T(8,128)(2,1)}, u32[]{:S(2)}) copy-start(bf16[64,192]{1,0:T(8,128)(2,1)} %constant.46.clone.refs_19_.ty) | copy-start | bytes 73732
